TPU v7x, 256 devices: a whole 4x4x8 slice. The times are simulated.
256 devices in a mesh: seq: 64 (over z, y, core), ch: 4 (over x).
Axes of the slice: x: 4, y: 4, z: 8, core: 2. Of those that a mesh axis runs over, the one named last changes fastest.
Arguments:
- signal: bfloat16 [32768, 1024], P('seq', 'ch'), may hold values from -6 to 6
- gate_values: bfloat16 [32768, 1024], P('seq', 'ch'), may hold values from -6 to 6
- cotangent: bfloat16 [32768, 1024], P('seq', 'ch'), may hold values from -6 to 6
- skip_gain: float32 [1024], P('ch'), may hold values from -3 to 3
- log_rate: float32 [1024], P('ch'), as said below
- embed_weight: float32 [33, 64], replicated, may hold values from -1 to 1
- sine_freq: float32 [64], replicated, may hold values from 1 to 8
- mid_weight: float32 [64, 64], replicated, may hold values from -0.75 to 0.75
- out_weight: float32 [64, 1024], P(None, 'ch'), may hold values from -0.75 to 0.75
Outputs:
- output: bfloat16 [32768, 1024], P('seq', 'ch')
- signal_grad: bfloat16 [32768, 1024], P('seq', 'ch')
- gate_grad: bfloat16 [32768, 1024], P('seq', 'ch')
- skip_grad: float32 [1024], P('ch')
- rate_grad: float32 [1024], P('ch')
- out_weight_grad: float32 [64, 1024], P(None, 'ch')
- embed_grad: float32 [33, 64], replicated
- mid_grad: float32 [64, 64], replicated
- freq_grad: float32 [64], replicated
Inputs may be any that keep to these rules, and one draw needn't show every extreme that they name: exp(log_rate) lies between 0.25 / 32768 and 1 / 30.
All inputs are finite; a program needn't handle non-finite values.
Results may differ from a plain program's by a relative error of at most 0.0051.
Values may be sent and summed in bfloat16 or wider, within the bound.
A program may use at most 128 MiB of HBM per device.

v0:
```python
from functools import partial
import math

import jax
import jax.numpy as jnp
from jax import lax
from jax.sharding import PartitionSpec as P

highest = lax.Precision.HIGHEST
phase_modulus = 4093
band_stride = 255


def unit_angle(product, modulus):
    return (product % modulus).astype(jnp.float32) * (2.0 * math.pi / modulus)


def position_features(positions, seq_total, band_count):
    band_steps = 1 + band_stride * jnp.arange(band_count, dtype=jnp.int32)
    angles = unit_angle(positions[:, None] * band_steps[None, :], phase_modulus)
    position_ramp = positions.astype(jnp.float32)[:, None] / seq_total
    return jnp.concatenate([position_ramp, jnp.cos(angles), jnp.sin(angles)], axis=1)


def lower_layers(features, embed_weight, sine_freq, mid_weight):
    first_pre = jnp.dot(
        features, embed_weight, precision=highest, preferred_element_type=jnp.float32
    )
    first_act = jnp.sin(sine_freq[None, :] * first_pre)
    second_pre = jnp.dot(
        first_act, mid_weight, precision=highest, preferred_element_type=jnp.float32
    )
    return jnp.sin(sine_freq[None, :] * second_pre)


def split_length(length):
    leading = 1
    for candidate in range(1, math.isqrt(length) + 1):
        if length % candidate == 0:
            leading = candidate
    return (leading, length // leading)


def dft_tables(size_left, size_right, modulus):
    left_index = jnp.arange(size_left, dtype=jnp.int32)
    right_index = jnp.arange(size_right, dtype=jnp.int32)
    angles = unit_angle(left_index[:, None] * right_index[None, :], modulus)
    return (jnp.cos(angles), jnp.sin(angles))


def einsum_high(pattern, matrix, values):
    return jnp.einsum(pattern, matrix, values, precision=highest)


def local_forward(real_part, imag_part):
    stacks, length, channels = real_part.shape
    leading, trailing = split_length(length)
    real_part = real_part.reshape(stacks, leading, trailing, channels)
    imag_part = imag_part.reshape(stacks, leading, trailing, channels)
    cos_lead, sin_lead = dft_tables(leading, leading, leading)
    step_real = einsum_high("ka,eabc->ekbc", cos_lead, real_part) + einsum_high(
        "ka,eabc->ekbc", sin_lead, imag_part
    )
    step_imag = einsum_high("ka,eabc->ekbc", cos_lead, imag_part) - einsum_high(
        "ka,eabc->ekbc", sin_lead, real_part
    )
    cos_mid, sin_mid = dft_tables(leading, trailing, length)
    cos_mid = cos_mid[None, :, :, None]
    sin_mid = sin_mid[None, :, :, None]
    turned_real = step_real * cos_mid + step_imag * sin_mid
    turned_imag = step_imag * cos_mid - step_real * sin_mid
    cos_tail, sin_tail = dft_tables(trailing, trailing, trailing)
    out_real = einsum_high("qb,ekbc->ekqc", cos_tail, turned_real) + einsum_high(
        "qb,ekbc->ekqc", sin_tail, turned_imag
    )
    out_imag = einsum_high("qb,ekbc->ekqc", cos_tail, turned_imag) - einsum_high(
        "qb,ekbc->ekqc", sin_tail, turned_real
    )
    return (out_real, out_imag)


def local_inverse(real_part, imag_part):
    stacks, leading, trailing, channels = real_part.shape
    length = leading * trailing
    cos_tail, sin_tail = dft_tables(trailing, trailing, trailing)
    step_real = einsum_high("bq,ekqc->ekbc", cos_tail, real_part) - einsum_high(
        "bq,ekqc->ekbc", sin_tail, imag_part
    )
    step_imag = einsum_high("bq,ekqc->ekbc", cos_tail, imag_part) + einsum_high(
        "bq,ekqc->ekbc", sin_tail, real_part
    )
    cos_mid, sin_mid = dft_tables(leading, trailing, length)
    cos_mid = cos_mid[None, :, :, None]
    sin_mid = sin_mid[None, :, :, None]
    turned_real = step_real * cos_mid - step_imag * sin_mid
    turned_imag = step_imag * cos_mid + step_real * sin_mid
    cos_lead, sin_lead = dft_tables(leading, leading, leading)
    out_real = einsum_high("ak,ekbc->eabc", cos_lead, turned_real) - einsum_high(
        "ak,ekbc->eabc", sin_lead, turned_imag
    )
    out_imag = einsum_high("ak,ekbc->eabc", cos_lead, turned_imag) + einsum_high(
        "ak,ekbc->eabc", sin_lead, turned_real
    )
    return (out_real.reshape(stacks, length, channels), out_imag.reshape(stacks, length, channels))


def section_tables(devices, fft_length):
    sources = jnp.arange(devices, dtype=jnp.int32)
    row_index = jnp.arange(2 * devices, dtype=jnp.int32)
    fwd_angles = unit_angle(row_index[:, None] * sources[None, :], 2 * devices)
    inv_angles = unit_angle(sources[:, None] * row_index[None, :], 2 * devices)
    cos_fwd = jnp.cos(fwd_angles)
    sin_fwd = -jnp.sin(fwd_angles)
    cos_inv = jnp.cos(inv_angles) / fft_length
    sin_inv = -jnp.sin(inv_angles) / fft_length
    return (cos_fwd, sin_fwd, cos_inv, sin_inv)


def on_device(
    signal,
    gate_values,
    cotangent,
    skip_gain,
    log_rate,
    embed_weight,
    sine_freq,
    mid_weight,
    out_weight,
):
    devices = lax.axis_size("seq")
    seq_index = lax.axis_index("seq")
    local_len, channels = signal.shape
    seq_total = devices * local_len
    fft_length = 2 * seq_total
    cos_fwd, sin_fwd, cos_inv, sin_inv = section_tables(devices, fft_length)
    column_index = jnp.arange(local_len, dtype=jnp.int32)
    positions = seq_index * local_len + column_index

    def section_forward(pieces):
        pieces = pieces.astype(jnp.float32)
        return (
            einsum_high("rs,sjc->rjc", cos_fwd, pieces),
            einsum_high("rs,sjc->rjc", sin_fwd, pieces),
        )

    def row_frequencies():
        return 2 * seq_index + jnp.arange(2, dtype=jnp.int32)

    def expand_rows(received):
        real_part, imag_part = received
        angles = unit_angle(row_frequencies()[:, None] * column_index[None, :], fft_length)[
            :, :, None
        ]
        cos_rows = jnp.cos(angles)
        sin_rows = jnp.sin(angles)
        rows_real = real_part * cos_rows + imag_part * sin_rows
        rows_imag = imag_part * cos_rows - real_part * sin_rows
        return local_forward(rows_real, rows_imag)

    def to_spectrum(columns):
        return expand_rows(
            (
                lax.all_to_all(columns[0], "seq", split_axis=0, concat_axis=1, tiled=True),
                lax.all_to_all(columns[1], "seq", split_axis=0, concat_axis=1, tiled=True),
            )
        )

    def section_inverse(received):
        real_part, imag_part = received
        return einsum_high("br,rjc->bjc", cos_inv, real_part) + einsum_high(
            "br,rjc->bjc", sin_inv, imag_part
        )

    def to_positions(spectrum):
        real_part, imag_part = local_inverse(spectrum[0], spectrum[1])
        angles = unit_angle(row_frequencies()[:, None] * column_index[None, :], fft_length)[
            :, :, None
        ]
        cos_rows = jnp.cos(angles)
        sin_rows = jnp.sin(angles)
        plain_real = real_part * cos_rows - imag_part * sin_rows
        plain_imag = imag_part * cos_rows + real_part * sin_rows
        packed = (plain_real, plain_imag)
        rows_back = section_inverse(
            (
                lax.all_to_all(packed[0], "seq", split_axis=1, concat_axis=0, tiled=True),
                lax.all_to_all(packed[1], "seq", split_axis=1, concat_axis=0, tiled=True),
            )
        )
        field = lax.all_to_all(rows_back, "seq", split_axis=0, concat_axis=1, tiled=True)
        return field[0]

    band_count = (embed_weight.shape[0] - 1) // 2
    features = position_features(positions, seq_total, band_count)
    upper_act, lower_pull = jax.vjp(
        partial(lower_layers, features), embed_weight, sine_freq, mid_weight
    )
    raw_filter = jnp.dot(
        upper_act, out_weight, precision=highest, preferred_element_type=jnp.float32
    )
    decay_rate = jnp.exp(log_rate)
    place = positions.astype(jnp.float32)[:, None]
    envelope = jnp.exp(-decay_rate[None, :] * place) * jnp.sqrt(2.0 * decay_rate)[None, :]
    signal_f = signal.astype(jnp.float32)
    gate_f = gate_values.astype(jnp.float32)
    cot_f = cotangent.astype(jnp.float32)
    upstream_bf = (cot_f * gate_f).astype(jnp.bfloat16)
    upstream = lax.optimization_barrier(upstream_bf).astype(jnp.float32)
    signal_cols = section_forward(
        lax.all_to_all(signal[None], "seq", split_axis=1, concat_axis=0, tiled=True)
    )
    kernel = raw_filter * envelope
    kernel_cols = section_forward(
        lax.all_to_all(kernel[None], "seq", split_axis=1, concat_axis=0, tiled=True)
    )
    signal_spec = to_spectrum(signal_cols)
    kernel_spec = to_spectrum(kernel_cols)
    conv_spec = (
        kernel_spec[0] * signal_spec[0] - kernel_spec[1] * signal_spec[1],
        kernel_spec[0] * signal_spec[1] + kernel_spec[1] * signal_spec[0],
    )
    conv_out = to_positions(conv_spec)
    upstream_cols = section_forward(
        lax.all_to_all(upstream_bf[None], "seq", split_axis=1, concat_axis=0, tiled=True)
    )
    upstream_spec = to_spectrum(upstream_cols)
    joined_real = jnp.concatenate(
        [
            kernel_spec[0] * upstream_spec[0] + kernel_spec[1] * upstream_spec[1],
            signal_spec[0] * upstream_spec[0] + signal_spec[1] * upstream_spec[1],
        ],
        axis=3,
    )
    joined_imag = jnp.concatenate(
        [
            kernel_spec[0] * upstream_spec[1] - kernel_spec[1] * upstream_spec[0],
            signal_spec[0] * upstream_spec[1] - signal_spec[1] * upstream_spec[0],
        ],
        axis=3,
    )
    back_fields = to_positions((joined_real, joined_imag))
    signal_corr = back_fields[:, :channels]
    kernel_grad = back_fields[:, channels:]
    mixed_sum = conv_out + skip_gain[None, :] * signal_f
    output = (gate_f * mixed_sum).astype(jnp.bfloat16)
    gate_grad = (cot_f * mixed_sum).astype(jnp.bfloat16)
    signal_grad = (skip_gain[None, :] * upstream + signal_corr).astype(jnp.bfloat16)
    skip_part = jnp.sum(upstream * signal_f, axis=0)
    rate_part = jnp.sum(
        kernel_grad * raw_filter * envelope * (0.5 - decay_rate[None, :] * place), axis=0
    )
    scaled_kernel = kernel_grad * envelope
    out_part = jnp.dot(
        upper_act.T, scaled_kernel, precision=highest, preferred_element_type=jnp.float32
    )
    upper_grad = jnp.dot(
        scaled_kernel, out_weight.T, precision=highest, preferred_element_type=jnp.float32
    )
    upper_grad = lax.psum(upper_grad, "ch")
    embed_part, freq_part, mid_part = lower_pull(upper_grad)
    out_sum, skip_sum, rate_sum, embed_sum, mid_sum, freq_sum = lax.psum(
        (out_part, skip_part, rate_part, embed_part, mid_part, freq_part), "seq"
    )
    grad_scale = 1.0 / math.sqrt(seq_total)
    return (
        output,
        signal_grad,
        gate_grad,
        skip_sum * grad_scale,
        rate_sum * grad_scale,
        out_sum * grad_scale,
        embed_sum * grad_scale,
        mid_sum * grad_scale,
        freq_sum * grad_scale,
    )


def solution(mesh):
    in_specs = (
        P("seq", "ch"),
        P("seq", "ch"),
        P("seq", "ch"),
        P("ch"),
        P("ch"),
        P(),
        P(),
        P(),
        P(None, "ch"),
    )
    out_specs = (
        P("seq", "ch"),
        P("seq", "ch"),
        P("seq", "ch"),
        P("ch"),
        P("ch"),
        P(None, "ch"),
        P(),
        P(),
        P(),
    )
    return jax.shard_map(
        on_device, mesh=mesh, in_specs=in_specs, out_specs=out_specs, check_vma=False
    )
```

profile of v0, /device:TPU:1, one launch (start us, length us, event | category | flops | bytes accessed | tf_op | source)
XLA Modules:
  0.0 1062.0 jit_solution(7820798269313045726)
XLA Ops:
  12.3 13.2 %all-to-all-start.9 = ((bf16[64,2,1024]{2,1,0:T(2,128)(2,1)}), bf16[64,2,1024]{2,1,0:T(2,128)(2,1)S(1)}, u32[]{:S(2)}, u32[]{:S(2)}) async-start(bf16[64,2,1024]{2,1,0:T(2,128)(2,1)} %reshape.243), calls=%async_computation.9 | async-start | bytes 524288 | tf_op jit(solution)/shard_map/all_to_all | solution.py:224
  30.3 8.3 all-to-all-done.9
  38.7 4.7 all-to-all-start.3
  46.6 10.0 all-to-all-done.3
  56.5 4.7 all-to-all-start
  63.9 15.0 %all-to-all-done = f32[1,512,256]{2,0,1:T(1,128)S(1)} async-done(((f32[1,512,256]{2,0,1:T(1,128)}), f32[1,512,256]{2,0,1:T(1,128)S(1)}, u32[]{:S(2)}, u32[]{:S(2)}) %all-to-all-start) | async-done | bytes 524320 | tf_op jit(solution)/shard_map/all_to_all | solution.py:214
  79.8 6.0 all-to-all-start.11
  88.2 25.6 %all-to-all-done.11 = f32[128,8,256]{2,1,0:T(8,128)S(1)} async-done(((f32[128,8,256]{2,1,0:T(8,128)}), f32[128,8,256]{2,1,0:T(8,128)S(1)}, u32[]{:S(2)}, u32[]{:S(2)}) %all-to-all-start.11) | async-done | bytes 1048608 | tf_op jit(solution)/shard_map/all_to_all | solution.py:164
  113.8 6.5 all-to-all-start.10
  124.7 23.6 %all-to-all-done.10 = f32[128,8,256]{2,1,0:T(8,128)S(1)} async-done(((f32[128,8,256]{2,1,0:T(8,128)}), f32[128,8,256]{2,1,0:T(8,128)S(1)}, u32[]{:S(2)}, u32[]{:S(2)}) %all-to-all-start.10) | async-done | bytes 1048608 | tf_op jit(solution)/shard_map/all_to_all | solution.py:163
  148.2 6.7 all-to-all-start.5
  157.2 25.6 %all-to-all-done.5 = f32[128,8,256]{2,1,0:T(8,128)} async-done(((f32[128,8,256]{2,1,0:T(8,128)}), f32[128,8,256]{2,1,0:T(8,128)}, u32[]{:S(2)}, u32[]{:S(2)}) %all-to-all-start.5) | async-done | bytes 1048608 | tf_op jit(solution)/shard_map/all_to_all | solution.py:164
  182.8 6.8 all-to-all-start.4
  192.4 25.1 %all-to-all-done.4 = f32[128,8,256]{2,1,0:T(8,128)} async-done(((f32[128,8,256]{2,1,0:T(8,128)}), f32[128,8,256]{2,1,0:T(8,128)}, u32[]{:S(2)}, u32[]{:S(2)}) %all-to-all-start.4) | async-done | bytes 1048608 | tf_op jit(solution)/shard_map/all_to_all | solution.py:163
  217.5 6.7 all-to-all-start.2
  226.9 25.1 %all-to-all-done.2 = f32[128,8,256]{2,1,0:T(8,128)} async-done(((f32[128,8,256]{2,1,0:T(8,128)}), f32[128,8,256]{2,1,0:T(8,128)}, u32[]{:S(2)}, u32[]{:S(2)}) %all-to-all-start.2) | async-done | bytes 1048608 | tf_op jit(solution)/shard_map/all_to_all | solution.py:164
  252.0 15.4 %all-to-all-start.1 = ((f32[128,8,256]{2,1,0:T(8,128)}), f32[128,8,256]{2,1,0:T(8,128)}, u32[]{:S(2)}, u32[]{:S(2)}) async-start(f32[128,8,256]{2,1,0:T(8,128)} %copy.247), calls=%async_computation.1 | async-start | bytes 2097152 | tf_op jit(solution)/shard_map/all_to_all | solution.py:163
  276.3 10.3 all-to-all-done.1
  356.1 6.7 all-to-all-start.6
  390.7 9.6 all-to-all-start.12
  403.2 46.4 %all-to-all-done.12 = f32[2,512,512]{2,0,1:T(2,128)} async-done(((f32[2,512,512]{2,0,1:T(2,128)}), f32[2,512,512]{2,0,1:T(2,128)}, u32[]{:S(2)}, u32[]{:S(2)}) %all-to-all-start.12) | async-done | bytes 2097184 | tf_op jit(solution)/shard_map/all_to_all | solution.py:186
  449.6 7.1 all-to-all-start.13
  459.7 46.7 %all-to-all-done.13 = f32[2,512,512]{2,0,1:T(2,128)S(1)} async-done(((f32[2,512,512]{2,0,1:T(2,128)}), f32[2,512,512]{2,0,1:T(2,128)S(1)}, u32[]{:S(2)}, u32[]{:S(2)}) %all-to-all-start.13) | async-done | bytes 2097184 | tf_op jit(solution)/shard_map/all_to_all | solution.py:187
  506.3 7.2 all-to-all-start.7
  533.9 7.6 all-to-all-done.7
  541.5 7.1 all-to-all-start.14
  559.2 17.0 %all-to-all-done.14 = f32[64,8,512]{2,1,0:T(8,128)} async-done(((f32[64,8,512]{2,1,0:T(8,128)}), f32[64,8,512]{2,1,0:T(8,128)}, u32[]{:S(2)}, u32[]{:S(2)}) %all-to-all-start.14) | async-done | bytes 1048608 | tf_op jit(solution)/shard_map/all_to_all | solution.py:190
  576.2 6.5 all-to-all-start.8
  588.0 12.4 %all-to-all-done.8 = f32[64,8,256]{2,1,0:T(8,128)S(1)} async-done(((f32[64,8,256]{2,1,0:T(8,128)}), f32[64,8,256]{2,1,0:T(8,128)S(1)}, u32[]{:S(2)}, u32[]{:S(2)}) %all-to-all-start.8) | async-done | bytes 524320 | tf_op jit(solution)/shard_map/all_to_all | solution.py:190
  603.0 153.4 %all-reduce.4.cloned.1.call-done = f32[64,256]{1,0:T(8,128)} async-done(((f32[64,256]{1,0:T(8,128)}), f32[64,256]{1,0:T(8,128)}) %all-reduce.4.cloned.1.call-update) | async-done | bytes 65552 | tf_op jit(solution)/shard_map/psum | solution.py:261
  757.9 41.9 %all-reduce.6.cloned.1.call-done = f32[512,64]{0,1:T(8,128)} async-done(((f32[512,64]{0,1:T(8,128)}), f32[512,64]{0,1:T(8,128)}) %all-reduce.6.cloned.1.call-update) | async-done | bytes 131088 | tf_op jit(solution)/shard_map/psum | solution.py:259
  805.8 246.1 %all-reduce = (f32[256]{0:T(256)S(1)}, f32[256]{0:T(256)S(1)}, f32[33,64]{1,0:T(8,128)S(1)}, f32[64,64]{1,0:T(8,128)S(1)}, f32[64]{0:T(128)S(1)}) all-reduce(f32[256]{0:T(256)S(1)} %get-tuple-element.48, f32[256]{0:T(256)S(1)} %get-tuple-element.44, f32[33,64]{1,0:T(8,128)S(1)} %fusion.114, ...), channel_id=1, replica_groups=mesh['seq'=64,'ch'=4] {'seq'}, use_global_device_ids=true, to_apply=%region_1.2 | all-reduce | flops 6784 | bytes 54272 | tf_op jit(solution)/shard_map/psum | solution.py:261
  (184 shorter events, 192.0 us)
Async XLA Ops:
  7.2 36.8 %copy-start = (f32[64,256]{1,0:T(8,128)S(1)}, f32[64,256]{1,0:T(8,128)}, u32[]{:S(2)}) copy-start(f32[64,256]{1,0:T(8,128)} %param.17) | copy-start | bytes 196612
  7.2 18.3 %copy-start.13 = (bf16[512,256]{1,0:T(8,128)(2,1)S(1)}, bf16[512,256]{1,0:T(8,128)(2,1)}, u32[]{:S(2)}) copy-start(bf16[512,256]{1,0:T(8,128)(2,1)} %param.9) | copy-start | bytes 786436
  8.8 20.5 %copy-start.18 = (f32[33,64]{1,0:T(8,128)S(1)}, f32[33,64]{1,0:T(8,128)}, u32[]{:S(2)}) copy-start(f32[33,64]{1,0:T(8,128)} %param.14) | copy-start | bytes 25348
  9.3 20.3 %copy-start.15 = (f32[64,64]{1,0:T(8,128)S(1)}, f32[64,64]{1,0:T(8,128)}, u32[]{:S(2)}) copy-start(f32[64,64]{1,0:T(8,128)} %param.16) | copy-start | bytes 49156
  9.3 20.3 %copy-start.17 = (f32[64]{0:T(128)S(1)}, f32[64]{0:T(128)}, u32[]{:S(2)}) copy-start(f32[64]{0:T(128)} %param.15) | copy-start | bytes 772
  11.5 31.9 %copy-start.22 = (f32[256]{0:T(256)S(1)}, f32[256]{0:T(256)}, u32[]{:S(2)}) copy-start(f32[256]{0:T(256)} %param.13) | copy-start | bytes 3076
  12.3 26.3 %all-to-all-start.9 = ((bf16[64,2,1024]{2,1,0:T(2,128)(2,1)}), bf16[64,2,1024]{2,1,0:T(2,128)(2,1)S(1)}, u32[]{:S(2)}, u32[]{:S(2)}) async-start(bf16[64,2,1024]{2,1,0:T(2,128)(2,1)} %reshape.243), calls=%async_computation.9 | async-start | bytes 524288 | tf_op jit(solution)/shard_map/all_to_all | solution.py:224
  38.7 17.9 %all-to-all-start.3 = ((bf16[64,2,1024]{2,1,0:T(2,128)(2,1)}), bf16[64,2,1024]{2,1,0:T(2,128)(2,1)S(1)}, u32[]{:S(2)}, u32[]{:S(2)}) async-start(bf16[64,2,1024]{2,1,0:T(2,128)(2,1)} %reshape.241), calls=%async_computation.3 | async-start | bytes 524288 | tf_op jit(solution)/shard_map/all_to_all | solution.py:210
  44.0 12.6 %copy-start.19 = (f32[256]{0:T(256)}, f32[256]{0:T(256)S(1)}, u32[]{:S(2)}) copy-start(f32[256]{0:T(256)S(1)} %get-tuple-element.65) | copy-start | bytes 3076
  56.5 22.4 %all-to-all-start = ((f32[1,512,256]{2,0,1:T(1,128)}), f32[1,512,256]{2,0,1:T(1,128)S(1)}, u32[]{:S(2)}, u32[]{:S(2)}) async-start(f32[1,512,256]{2,0,1:T(1,128)} %copy.245), calls=%async_computation | async-start | bytes 1048576 | tf_op jit(solution)/shard_map/all_to_all | solution.py:214
  79.8 34.0 %all-to-all-start.11 = ((f32[128,8,256]{2,1,0:T(8,128)}), f32[128,8,256]{2,1,0:T(8,128)S(1)}, u32[]{:S(2)}, u32[]{:S(2)}) async-start(f32[128,8,256]{2,1,0:T(8,128)} %copy.295), calls=%async_computation.11 | async-start | bytes 2097152 | tf_op jit(solution)/shard_map/all_to_all | solution.py:164
  86.5 33.7 %copy-start.10 = (bf16[64,2,1024]{2,1,0:T(2,128)(2,1)S(1)}, bf16[64,2,1024]{2,1,0:T(2,128)(2,1)}, u32[]{:S(2)}) copy-start(bf16[64,2,1024]{2,1,0:T(2,128)(2,1)} %copy-done.9) | copy-start | bytes 786436
  113.8 34.5 %all-to-all-start.10 = ((f32[128,8,256]{2,1,0:T(8,128)}), f32[128,8,256]{2,1,0:T(8,128)S(1)}, u32[]{:S(2)}, u32[]{:S(2)}) async-start(f32[128,8,256]{2,1,0:T(8,128)} %copy.292), calls=%async_computation.10 | async-start | bytes 2097152 | tf_op jit(solution)/shard_map/all_to_all | solution.py:163
  148.2 34.6 %all-to-all-start.5 = ((f32[128,8,256]{2,1,0:T(8,128)}), f32[128,8,256]{2,1,0:T(8,128)}, u32[]{:S(2)}, u32[]{:S(2)}) async-start(f32[128,8,256]{2,1,0:T(8,128)} %copy.265), calls=%async_computation.5 | async-start | bytes 2097152 | tf_op jit(solution)/shard_map/all_to_all | solution.py:164
  182.8 34.7 %all-to-all-start.4 = ((f32[128,8,256]{2,1,0:T(8,128)}), f32[128,8,256]{2,1,0:T(8,128)}, u32[]{:S(2)}, u32[]{:S(2)}) async-start(f32[128,8,256]{2,1,0:T(8,128)} %copy.262), calls=%async_computation.4 | async-start | bytes 2097152 | tf_op jit(solution)/shard_map/all_to_all | solution.py:163
  217.5 34.6 %all-to-all-start.2 = ((f32[128,8,256]{2,1,0:T(8,128)}), f32[128,8,256]{2,1,0:T(8,128)}, u32[]{:S(2)}, u32[]{:S(2)}) async-start(f32[128,8,256]{2,1,0:T(8,128)} %copy.250), calls=%async_computation.2 | async-start | bytes 2097152 | tf_op jit(solution)/shard_map/all_to_all | solution.py:164
  252.0 34.6 %all-to-all-start.1 = ((f32[128,8,256]{2,1,0:T(8,128)}), f32[128,8,256]{2,1,0:T(8,128)}, u32[]{:S(2)}, u32[]{:S(2)}) async-start(f32[128,8,256]{2,1,0:T(8,128)} %copy.247), calls=%async_computation.1 | async-start | bytes 2097152 | tf_op jit(solution)/shard_map/all_to_all | solution.py:163
  356.1 34.6 %all-to-all-start.6 = ((f32[2,512,256]{2,0,1:T(2,128)}), f32[2,512,256]{2,0,1:T(2,128)}, u32[]{:S(2)}, u32[]{:S(2)}) async-start(f32[2,512,256]{2,0,1:T(2,128)} %copy.283), calls=%async_computation.6 | async-start | bytes 2097152 | tf_op jit(solution)/shard_map/all_to_all | solution.py:186
  390.7 58.9 %all-to-all-start.12 = ((f32[2,512,512]{2,0,1:T(2,128)}), f32[2,512,512]{2,0,1:T(2,128)}, u32[]{:S(2)}, u32[]{:S(2)}) async-start(f32[2,512,512]{2,0,1:T(2,128)} %copy.311), calls=%async_computation.12 | async-start | bytes 4194304 | tf_op jit(solution)/shard_map/all_to_all | solution.py:186
  449.6 56.7 %all-to-all-start.13 = ((f32[2,512,512]{2,0,1:T(2,128)}), f32[2,512,512]{2,0,1:T(2,128)S(1)}, u32[]{:S(2)}, u32[]{:S(2)}) async-start(f32[2,512,512]{2,0,1:T(2,128)} %copy.314), calls=%async_computation.13 | async-start | bytes 4194304 | tf_op jit(solution)/shard_map/all_to_all | solution.py:187
  506.3 35.1 %all-to-all-start.7 = ((f32[2,512,256]{2,0,1:T(2,128)}), f32[2,512,256]{2,0,1:T(2,128)}, u32[]{:S(2)}, u32[]{:S(2)}) async-start(f32[2,512,256]{2,0,1:T(2,128)} %copy.286), calls=%async_computation.7 | async-start | bytes 2097152 | tf_op jit(solution)/shard_map/all_to_all | solution.py:187
  541.5 34.8 %all-to-all-start.14 = ((f32[64,8,512]{2,1,0:T(8,128)}), f32[64,8,512]{2,1,0:T(8,128)}, u32[]{:S(2)}, u32[]{:S(2)}) async-start(f32[64,8,512]{2,1,0:T(8,128)} %copy.317), calls=%async_computation.14 | async-start | bytes 2097152 | tf_op jit(solution)/shard_map/all_to_all | solution.py:190
  558.0 24.7 %copy-start.20 = (f32[256]{0:T(256)S(1)}, f32[256]{0:T(256)}, u32[]{:S(2)}) copy-start(f32[256]{0:T(256)} %copy-done.19) | copy-start | bytes 3076
  558.0 42.4 %copy-start.11 = (bf16[512,256]{1,0:T(8,128)(2,1)S(1)}, bf16[512,256]{1,0:T(8,128)(2,1)}, u32[]{:S(2)}) copy-start(bf16[512,256]{1,0:T(8,128)(2,1)} %param.10) | copy-start | bytes 786436
  558.0 42.4 %copy-start.12 = (bf16[512,256]{1,0:T(8,128)(2,1)S(1)}, bf16[512,256]{1,0:T(8,128)(2,1)}, u32[]{:S(2)}) copy-start(bf16[512,256]{1,0:T(8,128)(2,1)} %param.11) | copy-start | bytes 786436
  558.0 42.4 %copy-start.14 = (bf16[512,256]{1,0:T(8,128)(2,1)S(1)}, bf16[512,256]{1,0:T(8,128)(2,1)}, u32[]{:S(2)}) copy-start(bf16[512,256]{1,0:T(8,128)(2,1)} %param.9) | copy-start | bytes 786436
  558.1 42.4 %copy-start.21 = (f32[256]{0:T(256)S(1)}, f32[256]{0:T(256)}, u32[]{:S(2)}) copy-start(f32[256]{0:T(256)} %get-tuple-element.63) | copy-start | bytes 3076
  558.1 42.4 %copy-start.23 = (f32[256]{0:T(256)S(1)}, f32[256]{0:T(256)}, u32[]{:S(2)}) copy-start(f32[256]{0:T(256)} %param.12) | copy-start | bytes 3076
  576.2 24.2 %all-to-all-start.8 = ((f32[64,8,256]{2,1,0:T(8,128)}), f32[64,8,256]{2,1,0:T(8,128)S(1)}, u32[]{:S(2)}, u32[]{:S(2)}) async-start(f32[64,8,256]{2,1,0:T(8,128)} %copy.289), calls=%async_computation.8 | async-start | bytes 1048576 | tf_op jit(solution)/shard_map/all_to_all | solution.py:190
  582.7 173.7 %all-reduce.4.cloned.1.call-start = ((), (), s32[]{:S(2)}) async-start(), calls=%async_computation.15 | async-start | bytes 131072 | tf_op jit(solution)/shard_map/psum | solution.py:261
  585.4 214.3 %all-reduce.6.cloned.1.call-start = ((), (), s32[]{:S(2)}) async-start(), calls=%async_computation.16 | async-start | bytes 262144 | tf_op jit(solution)/shard_map/psum | solution.py:259
  588.0 211.8 %copy-start.16 = (f32[64,64]{1,0:T(8,128)S(1)}, f32[64,64]{1,0:T(8,128)}, u32[]{:S(2)}) copy-start(f32[64,64]{1,0:T(8,128)} %param.16) | copy-start | bytes 49156
  (9 other events, 34.4 us)
Sparse Core Ops, SparseCore 0:
  587.6 168.7 all-reduce.3
  758.7 41.0 all-reduce.5
where the time goes:
time: 1080 us; the launch traced here: 1060 us
  waiting for transfers between devices  495 us (46%)
  blocking collectives  246 us (23%)
  starting transfers between devices  115 us (11%)
  matrix products  102 us (9%)
  local copies, waits for them, and re-layouts  69 us (6%)
  other arithmetic  19.3 us (2%)
  between operations  15.4 us (1%)
    psum x1, blocking collectives, on_device(): lax.psum((out_part, skip_part, rate_part, embed_part, mid_part, freq_part...  246 us
    psum x1, waiting for transfers between devices, on_device(): lax.psum((out_part, skip_part, rate_part, embed_part, mid_part, freq_part...  153 us
    dot_general x50, matrix products, einsum_high(): return jnp.einsum(pattern, matrix, values, precision=highest)  90.5 us
    all_to_all x3, waiting for transfers between devices, to_spectrum(): lax.all_to_all(columns[1], 'seq', split_axis=0, concat_axis=1, tiled=True)  76.3 us
    all_to_all x3, waiting for transfers between devices, to_spectrum(): lax.all_to_all(columns[0], 'seq', split_axis=0, concat_axis=1, tiled=True)  59 us
    all_to_all x2, waiting for transfers between devices, to_positions(): lax.all_to_all(packed[1], 'seq', split_axis=1, concat_axis=0, tiled=True)  54.2 us
    all_to_all x2, waiting for transfers between devices, to_positions(): lax.all_to_all(packed[0], 'seq', split_axis=1, concat_axis=0, tiled=True)  47.7 us
    psum x1, waiting for transfers between devices, on_device(): upper_grad = lax.psum(upper_grad, 'ch')  41.9 us
  transfers between devices with their start and end apart: 17, of which 17 were waited for; matrix products, arithmetic and copies ran while one was open for 9% of the time, Pallas kernels for 0%

commit v1 on v0

v1 whole, which is shorter than its diff:
```python
import math
from functools import partial

import jax
import jax.numpy as jnp
import ml_dtypes
import numpy as np
from jax import lax
from jax.experimental import pallas as pl
from jax.experimental.pallas import tpu as pltpu
from jax.sharding import PartitionSpec as P

MESH = pl.DeviceIdType.MESH
HIGH = lax.Precision.HIGHEST
F32 = jnp.float32
BF16 = jnp.bfloat16

SHARDS = 64
LOC = 512
CH = 256
SEQ = SHARDS * LOC
GROUP = CH // SHARDS
QUARTERS = LOC // 128
CHUNK = GROUP * QUARTERS
ROWS = SHARDS * CHUNK
LEAD, TAIL = 256, 128
ORDER, BANDS = 64, 16
MODULUS, STRIDE = 4093, 255
OWNERS = 32
SCALE = 1.0 / math.sqrt(SEQ)

VM = pl.BlockSpec(memory_space=pltpu.VMEM)


def split_bf16(table):
    high = table.astype(np.float32).astype(ml_dtypes.bfloat16)
    low = (table - high.astype(np.float64)).astype(np.float32).astype(ml_dtypes.bfloat16)
    return np.stack([high, low])


def transform_tables():
    lead = np.arange(LEAD)
    tail = np.arange(TAIL)
    ang1 = 2 * np.pi * ((4 * lead[:, None] + 1) * lead[None, :] % (4 * LEAD)) / (4 * LEAD)
    first = np.concatenate([np.cos(ang1), -np.sin(ang1)], axis=0)
    last = np.concatenate([np.cos(ang1).T, -np.sin(ang1).T], axis=1)
    ang2 = 2 * np.pi * (tail[:, None] * tail[None, :] % TAIL) / TAIL
    cos2, sin2 = np.cos(ang2), np.sin(ang2)
    fwd2 = np.block([[cos2, -sin2], [sin2, cos2]])
    inv2 = np.block([[cos2, sin2], [-sin2, cos2]])
    angt = 2 * np.pi * ((4 * lead[:, None] + 1) * tail[None, :]) / (4 * SEQ)
    turn = np.stack([np.cos(angt), np.sin(angt)]).astype(np.float32)
    return tuple(split_bf16(t) for t in (first, last, fwd2, inv2)) + (turn,)


def dot_t(left, right, dims, precision=HIGH):
    return lax.dot_general(
        left, right, (dims, ((), ())), precision=precision, preferred_element_type=F32
    )


def column(row):
    size = row.shape[1]
    r = lax.broadcasted_iota(jnp.int32, (size, size), 0)
    c = lax.broadcasted_iota(jnp.int32, (size, size), 1)
    return jnp.sum(jnp.where(r == c, row, 0.0), axis=1, keepdims=True)


def spread(blocks, wide, out):
    for q in range(QUARTERS):
        block = blocks(q)
        for j in range(GROUP):
            wide[pl.ds(GROUP * q + j, SHARDS, stride=CHUNK), :] = block[
                SHARDS * j : SHARDS * (j + 1)
            ]
    out[...] = wide[...].astype(BF16)


def gather_quarter(wide, q):
    return jnp.concatenate(
        [wide[pl.ds(GROUP * q + j, SHARDS, stride=CHUNK), :] for j in range(GROUP)], axis=0
    )


def pre_kernel(
    sig_ref, gate_ref, cot_ref, logr_ref, emb_ref, freq_ref, mid_ref, outw_ref,
    sig_send, up_send, ker_send, env_ref, raw_ref, feat_ref, h1_ref, a1_ref, h2_ref, a2_ref, skip_ref,
    wide, emb_pad,
):
    seq_index = lax.axis_index("seq")
    sig = sig_ref[...].astype(F32)
    up = (cot_ref[...].astype(F32) * gate_ref[...].astype(F32)).astype(BF16).astype(F32)
    skip_ref[...] = jnp.sum(sig * up, axis=0, keepdims=True)
    spread(lambda q: jnp.transpose(sig[128 * q : 128 * (q + 1)]), wide, sig_send)
    spread(lambda q: jnp.transpose(up[128 * q : 128 * (q + 1)]), wide, up_send)

    base = seq_index * LOC
    pos = base + lax.broadcasted_iota(jnp.int32, (1, LOC), 1)
    band = 1 + STRIDE * lax.broadcasted_iota(jnp.int32, (BANDS, LOC), 0)
    prod = (base + lax.broadcasted_iota(jnp.int32, (BANDS, LOC), 1)) * band
    quot = (prod.astype(F32) * (1.0 / MODULUS)).astype(jnp.int32)
    rem = prod - quot * MODULUS
    rem = jnp.where(rem < 0, rem + MODULUS, rem)
    rem = jnp.where(rem >= MODULUS, rem - MODULUS, rem)
    angle = rem.astype(F32) * (2.0 * math.pi / MODULUS)
    place = pos.astype(F32)
    feat_ref[...] = jnp.zeros_like(feat_ref)
    feat_ref[0:1, :] = place / SEQ
    feat_ref[1 : 1 + BANDS, :] = jnp.cos(angle)
    feat_ref[1 + BANDS : 1 + 2 * BANDS, :] = jnp.sin(angle)
    emb_pad[...] = jnp.zeros_like(emb_pad)
    emb_pad[0 : 1 + 2 * BANDS, :] = emb_ref[...]
    freq = column(freq_ref[...])
    h1 = dot_t(emb_pad[...], feat_ref[...], ((0,), (0,)))
    a1 = jnp.sin(freq * h1)
    h2 = dot_t(mid_ref[...], a1, ((0,), (0,)))
    a2 = jnp.sin(freq * h2)
    h1_ref[...], a1_ref[...], h2_ref[...], a2_ref[...] = h1, a1, h2, a2
    raw = dot_t(outw_ref[...], a2, ((0,), (0,)))
    raw_ref[...] = raw
    rate = jnp.exp(column(logr_ref[...]))
    env = jnp.exp(-rate * place) * jnp.sqrt(2.0 * rate)
    env_ref[...] = env
    kern = raw * env
    spread(lambda q: kern[:, 128 * q : 128 * (q + 1)], wide, ker_send)


def fft_kernel(
    sig_ref, up_ref, ker_ref, first_ref, last_ref, fwd2_ref, inv2_ref, turn_ref,
    kg_send, conv_send, corr_send,
    wide, mid_buf, spec_s, spec_u, spec_k,
):
    def dot2(left_pair, right):
        return jnp.dot(left_pair[0], right, preferred_element_type=F32) + jnp.dot(
            left_pair[1], right, preferred_element_type=F32
        )

    def forward(src, spec):
        wide[...] = src[...].astype(F32)
        seqs = jnp.concatenate(
            [wide[pl.ds(j, LEAD, stride=GROUP), :].astype(BF16) for j in range(GROUP)], axis=1
        )
        cos, sin = turn_ref[0], turn_ref[1]
        step = dot2((first_ref[0], first_ref[1]), seqs)
        for j in range(GROUP):
            re = step[:LEAD, TAIL * j : TAIL * (j + 1)]
            im = step[LEAD:, TAIL * j : TAIL * (j + 1)]
            mid_buf[LEAD * j : LEAD * (j + 1), :TAIL] = (re * cos + im * sin).astype(BF16)
            mid_buf[LEAD * j : LEAD * (j + 1), TAIL:] = (im * cos - re * sin).astype(BF16)
        turned = mid_buf[...]
        spec[...] = jnp.dot(turned, fwd2_ref[0], preferred_element_type=F32) + jnp.dot(
            turned, fwd2_ref[1], preferred_element_type=F32
        )

    def inverse(left, right, conj_left, out):
        lr, li = left[:, :TAIL], left[:, TAIL:]
        rr, ri = right[:, :TAIL], right[:, TAIL:]
        if conj_left:
            re, im = lr * rr + li * ri, lr * ri - li * rr
        else:
            re, im = lr * rr - li * ri, lr * ri + li * rr
        mid_buf[:, :TAIL] = re.astype(BF16)
        mid_buf[:, TAIL:] = im.astype(BF16)
        spec = mid_buf[...]
        step = jnp.dot(spec, inv2_ref[0], preferred_element_type=F32) + jnp.dot(
            spec, inv2_ref[1], preferred_element_type=F32
        )
        cos, sin = turn_ref[0], turn_ref[1]
        reals, imags = [], []
        for j in range(GROUP):
            re = step[LEAD * j : LEAD * (j + 1), :TAIL]
            im = step[LEAD * j : LEAD * (j + 1), TAIL:]
            reals.append((re * cos - im * sin).astype(BF16))
            imags.append((im * cos + re * sin).astype(BF16))
        both = jnp.concatenate(
            [jnp.concatenate(reals, axis=1), jnp.concatenate(imags, axis=1)], axis=0
        )
        field = dot2((last_ref[0], last_ref[1]), both) * (1.0 / SEQ)
        for j in range(GROUP):
            wide[pl.ds(j, LEAD, stride=GROUP), :] = field[:, TAIL * j : TAIL * (j + 1)]
        out[...] = wide[...].astype(BF16)

    forward(sig_ref, spec_s)
    forward(up_ref, spec_u)
    inverse(spec_s, spec_u, True, kg_send)
    forward(ker_ref, spec_k)
    inverse(spec_k, spec_s, False, conv_send)
    inverse(spec_k, spec_u, True, corr_send)


def post_kernel(
    kg_ref, conv_ref, corr_ref, sig_ref, gate_ref, cot_ref, gain_ref, logr_ref, freq_ref, mid_ref, outw_ref,
    env_ref, raw_ref, feat_ref, h1_ref, a1_ref, h2_ref, a2_ref, skip_ref,
    out_ref, sgrad_ref, ggrad_ref, pack_ref,
    wide,
):
    place = (lax.axis_index("seq") * LOC + lax.broadcasted_iota(jnp.int32, (1, LOC), 1)).astype(F32)
    wide[...] = kg_ref[...].astype(F32)
    kgrad = jnp.concatenate([gather_quarter(wide, q) for q in range(QUARTERS)], axis=1)
    scaled = kgrad * env_ref[...]
    rate = jnp.exp(column(logr_ref[...]))
    weighted = scaled * raw_ref[...] * (0.5 - rate * place)
    ones = jnp.ones((8, LOC), F32)
    rate_part = dot_t(ones, weighted, ((1,), (1,)))[0:1]
    a2 = a2_ref[...]
    out_part = dot_t(a2, scaled, ((1,), (1,)))
    g2 = jnp.dot(outw_ref[...], scaled, precision=HIGH, preferred_element_type=F32)
    freq = column(freq_ref[...])
    h1, h2, a1 = h1_ref[...], h2_ref[...], a1_ref[...]
    c2 = jnp.cos(freq * h2) * g2
    d2 = freq * c2
    mid_part = dot_t(a1, d2, ((1,), (1,)))
    g1 = jnp.dot(mid_ref[...], d2, precision=HIGH, preferred_element_type=F32)
    c1 = jnp.cos(freq * h1) * g1
    d1 = freq * c1
    emb_part = dot_t(feat_ref[...], d1, ((1,), (1,)))
    freq_part = dot_t(ones, c2 * h2 + c1 * h1, ((1,), (1,)))[0:1]

    pack_ref[...] = jnp.zeros_like(pack_ref)
    pack_ref[pl.ds(0, 64, stride=4), :] = out_part[:, :128]
    pack_ref[pl.ds(1, 64, stride=4), :] = out_part[:, 128:]
    emb_cols = jnp.concatenate(
        [emb_part, jnp.broadcast_to(freq_part, (8, ORDER)), jnp.zeros((16, ORDER), F32)], axis=0
    )
    pack_ref[pl.ds(2, 64, stride=4), :] = jnp.concatenate([mid_part, emb_cols], axis=1)
    skip = skip_ref[...]
    pack_ref[3:4, :] = skip[:, :128]
    pack_ref[7:8, :] = skip[:, 128:]
    pack_ref[11:12, :] = rate_part[:, :128]
    pack_ref[15:16, :] = rate_part[:, 128:]

    gain = gain_ref[...]
    wide[...] = conv_ref[...].astype(F32)
    for q in range(QUARTERS):
        rows = slice(128 * q, 128 * (q + 1))
        conv = jnp.transpose(gather_quarter(wide, q))
        mixed = conv + gain * sig_ref[rows].astype(F32)
        gate = gate_ref[rows].astype(F32)
        cot = cot_ref[rows].astype(F32)
        out_ref[rows] = (gate * mixed).astype(BF16)
        ggrad_ref[rows] = (cot * mixed).astype(BF16)
    wide[...] = corr_ref[...].astype(F32)
    for q in range(QUARTERS):
        rows = slice(128 * q, 128 * (q + 1))
        corr = jnp.transpose(gather_quarter(wide, q))
        up = (cot_ref[rows].astype(F32) * gate_ref[rows].astype(F32)).astype(BF16).astype(F32)
        sgrad_ref[rows] = (gain * up + corr).astype(BF16)


def meet_seq(me, extra=()):
    barrier = pltpu.get_barrier_semaphore()

    def greet(i, carry):
        pl.semaphore_signal(
            barrier, inc=1, device_id={"seq": lax.rem(me + i, SHARDS)}, device_id_type=MESH
        )
        return carry

    lax.fori_loop(1, SHARDS, greet, 0)
    for peer in extra:
        pl.semaphore_signal(barrier, inc=1, device_id={"ch": peer}, device_id_type=MESH)
    pl.semaphore_wait(barrier, SHARDS - 1 + len(extra))


def exchange_kernel(count, *refs):
    sends, recvs = refs[:count], refs[count : 2 * count]
    send_sem, recv_sem, own_sem = refs[2 * count :]
    me = lax.axis_index("seq")
    meet_seq(me)
    mine = pl.ds(pl.multiple_of(me * CHUNK, CHUNK), CHUNK)

    for f in range(count):
        def push(i, carry, f=f):
            peer = lax.rem(me + i, SHARDS)
            theirs = pl.ds(pl.multiple_of(peer * CHUNK, CHUNK), CHUNK)
            pltpu.make_async_remote_copy(
                src_ref=sends[f].at[theirs],
                dst_ref=recvs[f].at[mine],
                send_sem=send_sem.at[f],
                recv_sem=recv_sem.at[f],
                device_id={"seq": peer},
                device_id_type=MESH,
            ).start()
            return carry

        lax.fori_loop(1, SHARDS, push, 0)
        pltpu.make_async_copy(sends[f].at[mine], recvs[f].at[mine], own_sem.at[f]).start()
    for f in range(count):
        rest = pl.ds(0, ROWS - CHUNK)
        done = pltpu.make_async_remote_copy(
            src_ref=sends[f].at[rest],
            dst_ref=recvs[f].at[rest],
            send_sem=send_sem.at[f],
            recv_sem=recv_sem.at[f],
            device_id={"seq": me},
            device_id_type=MESH,
        )
        done.wait_send()
        done.wait_recv()
        pltpu.make_async_copy(sends[f].at[mine], recvs[f].at[mine], own_sem.at[f]).wait()


def exchange(fields, collective_id):
    count = len(fields)
    return pl.pallas_call(
        partial(exchange_kernel, count),
        out_shape=[jax.ShapeDtypeStruct((ROWS, 128), BF16)] * count,
        in_specs=[VM] * count,
        out_specs=[VM] * count,
        scratch_shapes=[pltpu.SemaphoreType.DMA((count,))] * 3,
        compiler_params=pltpu.CompilerParams(collective_id=collective_id, has_side_effects=True),
        name="exchange%d" % collective_id,
    )(*fields)


def reduce_kernel(
    pack_ref, out_ref, skip_ref, rate_ref, emb_ref, mid_ref, freq_ref,
    parts, mine_buf, cross, total, sems,
):
    me = lax.axis_index("seq")
    lane = lax.axis_index("ch")
    others = [lax.rem(lane + i, 4) for i in (1, 2, 3)]
    meet_seq(me, others)
    owner = lax.div(me, 2)
    own_rows = pl.ds(pl.multiple_of(owner * 8, 8), 8)
    is_owner = lax.rem(me, 2) == 0

    def push(i, carry):
        slot = lax.rem(owner + i, OWNERS)
        pltpu.make_async_remote_copy(
            src_ref=pack_ref.at[pl.ds(pl.multiple_of(slot * 8, 8), 8)],
            dst_ref=parts.at[me],
            send_sem=sems.at[0],
            recv_sem=sems.at[1],
            device_id={"seq": 2 * slot},
            device_id_type=MESH,
        ).start()
        return carry

    lax.fori_loop(1, OWNERS, push, 0)

    @pl.when(jnp.logical_not(is_owner))
    def _():
        push(0, 0)

    def recv_rows(n, send, recv):
        return pltpu.make_async_remote_copy(
            src_ref=parts.at[pl.ds(0, n)],
            dst_ref=parts.at[pl.ds(0, n)],
            send_sem=sems.at[send],
            recv_sem=sems.at[recv],
            device_id={"seq": me},
            device_id_type=MESH,
        )

    @pl.when(is_owner)
    def _():
        recv_rows(SHARDS - 1, 0, 1).wait_recv()
        parts[me] = pack_ref[own_rows]
        acc = parts[0]
        for s in range(1, SHARDS):
            acc = acc + parts[s]
        mine_buf[...] = acc
        for n, other in enumerate(others):
            pltpu.make_async_remote_copy(
                src_ref=mine_buf,
                dst_ref=cross.at[2 - n],
                send_sem=sems.at[2],
                recv_sem=sems.at[3],
                device_id={"ch": other},
                device_id_type=MESH,
            ).start()
        recv_rows(3, 2, 3).wait_recv()
        shared = lax.rem(lax.broadcasted_iota(jnp.int32, (8, 128), 0), 4) == 2
        acc = acc + jnp.where(shared, cross[0] + cross[1] + cross[2], 0.0)
        total[own_rows] = acc
        recv_rows(3, 2, 3).wait_send()

        def tell(i, carry):
            pltpu.make_async_remote_copy(
                src_ref=total.at[own_rows],
                dst_ref=total.at[own_rows],
                send_sem=sems.at[4],
                recv_sem=sems.at[5],
                device_id={"seq": lax.rem(me + i, SHARDS)},
                device_id_type=MESH,
            ).start()
            return carry

        lax.fori_loop(1, SHARDS, tell, 0)
        recv_rows(OWNERS - 1, 4, 5).wait_recv()
        recv_rows(SHARDS - 1, 4, 5).wait_send()
        recv_rows(OWNERS - 1, 0, 1).wait_send()

    @pl.when(jnp.logical_not(is_owner))
    def _():
        recv_rows(OWNERS, 0, 1).wait_send()
        recv_rows(OWNERS, 4, 5).wait_recv()

    out_ref[:, :128] = total[pl.ds(0, 64, stride=4), :] * SCALE
    out_ref[:, 128:] = total[pl.ds(1, 64, stride=4), :] * SCALE
    shared_rows = total[pl.ds(2, 64, stride=4), :] * SCALE
    mid_ref[...] = shared_rows[:, :ORDER]
    emb_ref[...] = shared_rows[: 1 + 2 * BANDS, ORDER:]
    freq_ref[...] = shared_rows[40:41, ORDER:]
    skip_ref[:, :128] = total[3:4, :] * SCALE
    skip_ref[:, 128:] = total[7:8, :] * SCALE
    rate_ref[:, :128] = total[11:12, :] * SCALE
    rate_ref[:, 128:] = total[15:16, :] * SCALE


def reduce_params(pack):
    shapes = [(ORDER, CH), (1, CH), (1, CH), (1 + 2 * BANDS, ORDER), (ORDER, ORDER), (1, ORDER)]
    return pl.pallas_call(
        reduce_kernel,
        out_shape=[jax.ShapeDtypeStruct(s, F32) for s in shapes],
        in_specs=[VM],
        out_specs=[VM] * len(shapes),
        scratch_shapes=[
            pltpu.VMEM((SHARDS, 8, 128), F32),
            pltpu.VMEM((8, 128), F32),
            pltpu.VMEM((3, 8, 128), F32),
            pltpu.VMEM((256, 128), F32),
            pltpu.SemaphoreType.DMA((6,)),
        ],
        compiler_params=pltpu.CompilerParams(collective_id=3, has_side_effects=True),
        name="reduce_params",
    )(pack)


def on_device(signal, gate_values, cotangent, skip_gain, log_rate, embed_weight, sine_freq, mid_weight, out_weight):
    field = jax.ShapeDtypeStruct((ROWS, 128), BF16)
    full = jax.ShapeDtypeStruct((CH, LOC), F32)
    hidden = jax.ShapeDtypeStruct((ORDER, LOC), F32)
    gain, logr, freq = skip_gain[None, :], log_rate[None, :], sine_freq[None, :]
    pre = pl.pallas_call(
        pre_kernel,
        out_shape=[field] * 3
        + [full] * 2
        + [jax.ShapeDtypeStruct((40, LOC), F32)]
        + [hidden] * 4
        + [jax.ShapeDtypeStruct((1, CH), F32)],
        in_specs=[VM] * 8,
        out_specs=[VM] * 11,
        scratch_shapes=[pltpu.VMEM((ROWS, 128), F32), pltpu.VMEM((40, ORDER), F32)],
        name="pre",
    )(signal, gate_values, cotangent, logr, embed_weight, freq, mid_weight, out_weight)
    sends, kept = pre[:3], pre[3:]
    recvs = exchange(sends, 1)
    tables = transform_tables()
    fields = pl.pallas_call(
        fft_kernel,
        out_shape=[field] * 3,
        in_specs=[VM] * 8,
        out_specs=[VM] * 3,
        scratch_shapes=[pltpu.VMEM((ROWS, 128), F32), pltpu.VMEM((ROWS, 256), BF16)]
        + [pltpu.VMEM((ROWS, 256), F32)] * 3,
        name="transform",
    )(*recvs, *tables)
    back = exchange(fields, 2)
    wide_out = jax.ShapeDtypeStruct((LOC, CH), BF16)
    output, signal_grad, gate_grad, pack = pl.pallas_call(
        post_kernel,
        out_shape=[wide_out] * 3 + [jax.ShapeDtypeStruct((256, 128), F32)],
        in_specs=[VM] * 19,
        out_specs=[VM] * 4,
        scratch_shapes=[pltpu.VMEM((ROWS, 128), F32)],
        name="post",
    )(*back, signal, gate_values, cotangent, gain, logr, freq, mid_weight, out_weight, *kept)
    out_sum, skip_sum, rate_sum, emb_sum, mid_sum, freq_sum = reduce_params(pack)
    return (
        output, signal_grad, gate_grad, skip_sum[0], rate_sum[0], out_sum, emb_sum, mid_sum, freq_sum[0],
    )


def solution(mesh):
    wide, flat, rep = P("seq", "ch"), P("ch"), P()
    return jax.shard_map(
        on_device,
        mesh=mesh,
        in_specs=(wide, wide, wide, flat, flat, rep, rep, rep, P(None, "ch")),
        out_specs=(wide, wide, wide, flat, flat, P(None, "ch"), rep, rep, rep),
        check_vma=False,
    )
```

time: 1080 us -> 114 us (0.11); the launches traced: 1060 us -> 114 us
  waiting for transfers between devices: 495 us -> 0 us
  blocking collectives: 246 us -> 0 us
  starting transfers between devices: 115 us -> 0 us
  Pallas kernels: 0 us -> 108 us
  matrix products: 102 us -> 0 us
  local copies, waits for them, and re-layouts: 69 us -> 5.29 us
  other arithmetic: 19.3 us -> 0 us
  between operations: 15.4 us -> 0.69 us
    all_to_all x15 -> x0, waiting for transfers between devices: 300 us -> none  [the longest x3 76.3 us: to_spectrum(): lax.all_to_all(columns[1], 'seq', split_axis=0, concat_axis=1, tiled=True)]
    psum x1 -> x0, blocking collectives: 246 us -> none  [on_device(): lax.psum((out_part, skip_part, rate_part, embed_part, mid_part, freq_part...]
    psum x2 -> x0, waiting for transfers between devices: 195 us -> none  [the longest x1 153 us: on_device(): lax.psum((out_part, skip_part, rate_part, embed_part, mid_part, freq_part...]
    all_to_all x15 -> x0, starting transfers between devices: 115 us -> none  [the longest x3 28.6 us: to_spectrum(): lax.all_to_all(columns[0], 'seq', split_axis=0, concat_axis=1, tiled=True)]
    pallas_call x0 -> x6, Pallas kernels: none -> 108 us  [the longest x2 60.9 us: exchange(): pl.pallas_call(partial(exchange_kernel, count), out_shape=[jax.ShapeDtype...]
    dot_general x58 -> x0, matrix products: 102 us -> none  [the longest x50 90.5 us: einsum_high(): return jnp.einsum(pattern, matrix, values, precision=highest)]
    all_to_all x18 -> x0, local copies, waits for them, and re-layouts: 33.3 us -> none  [the longest x6 12.2 us: to_positions(): lax.all_to_all(packed[1], 'seq', split_axis=1, concat_axis=0, tiled=True)]
  transfers between devices with their start and end apart: 17 -> 0, of which waited for: 17 -> 0; matrix products, arithmetic and copies ran while one was open for 9% -> 0% of each run, Pallas kernels for 0% -> 0%
where the time goes in v1:
time: 114 us
  Pallas kernels  108 us (95%)
  local copies, waits for them, and re-layouts  5.29 us (5%)
    pallas_call x2, Pallas kernels, exchange(): pl.pallas_call(partial(exchange_kernel, count), out_shape=[jax.ShapeDtype...  60.9 us
    pallas_call x1, Pallas kernels, reduce_params(): pl.pallas_call(reduce_kernel, out_shape=[jax.ShapeDtypeStruct(s, F32) for...  28.5 us
    pallas_call x1, Pallas kernels, on_device(): pl.pallas_call(fft_kernel, out_shape=[field] * 3, in_specs=[VM] * 8, out_...  8.09 us
    pallas_call x1, Pallas kernels, on_device(): pl.pallas_call(post_kernel, out_shape=[wide_out] * 3 + [jax.ShapeDtypeStr...  5.78 us
    unnamed x16, local copies, waits for them, and re-layouts  5.29 us
    pallas_call x1, Pallas kernels, on_device(): pl.pallas_call(pre_kernel, out_shape=[field] * 3 + [full] * 2 + [jax.Shap...  4.59 us

profile of v1, /device:TPU:1, one launch (start us, length us, event | category | flops | bytes accessed | tf_op | source)
XLA Modules:
  0.0 113.8 jit_solution(12847779849746609953)
XLA Ops:
  0.6 4.6 %pre.1 = (bf16[1024,128]{1,0:T(8,128)(2,1)}, bf16[1024,128]{1,0:T(8,128)(2,1)}, bf16[1024,128]{1,0:T(8,128)(2,1)}, f32[256,512]{1,0:T(8,128)}, f32[256,512]{1,0:...) custom-call(bf16[512,256]{1,0:T(8,128)(2,1)} %sig_ref.3, ...), custom_call_target="tpu_custom_call" | custom-call | tf_op jit(solution)/shard_map/pre/pallas_call | solution.py:436
  5.2 32.6 %exchange1.1 = (bf16[1024,128]{1,0:T(8,128)(2,1)}, bf16[1024,128]{1,0:T(8,128)(2,1)}, bf16[1024,128]{1,0:T(8,128)(2,1)}) custom-call(bf16[1024,128]{1,0:T(8,128)(2,1)} %get-tuple-element.39.refs_0_, bf16[1024,128]{1,0:T(8,128)(2,1)} %get-tuple-element.40.refs_1_, bf16[1024,128]{1,0:T(8,128)(2,1)} %get-tuple-element.41.refs_2_), custom_call_target="tpu_custom_call" | custom-call | tf_op jit(solution)/shard_map/exchange1/pallas_call | solution.py:305
  37.9 8.1 %transform.1 = (bf16[1024,128]{1,0:T(8,128)(2,1)}, bf16[1024,128]{1,0:T(8,128)(2,1)}, bf16[1024,128]{1,0:T(8,128)(2,1)}) custom-call(bf16[1024,128]{1,0:T(8,128)(2,1)} %get-tuple-element.42.sig_ref, bf16[1024,128]{1,0:T(8,128)(2,1)} %get-tuple-element.43.up_ref, bf16[1024,128]{1,0:T(8,128)(2,1)} %get-tuple-element.44.ker_ref, ...), custom_call_target="tpu_custom_call" | custom-call | tf_op jit(solution)/shard_map/transform/pallas_call | solution.py:451
  46.0 28.2 %exchange2.1 = (bf16[1024,128]{1,0:T(8,128)(2,1)}, bf16[1024,128]{1,0:T(8,128)(2,1)}, bf16[1024,128]{1,0:T(8,128)(2,1)}) custom-call(bf16[1024,128]{1,0:T(8,128)(2,1)} %get-tuple-element.45.refs_0_, bf16[1024,128]{1,0:T(8,128)(2,1)} %get-tuple-element.46.refs_1_, bf16[1024,128]{1,0:T(8,128)(2,1)} %get-tuple-element.47.refs_2_), custom_call_target="tpu_custom_call" | custom-call | tf_op jit(solution)/shard_map/exchange2/pallas_call | solution.py:305
  74.2 5.8 %post.1 = (bf16[512,256]{1,0:T(8,128)(2,1)}, bf16[512,256]{1,0:T(8,128)(2,1)}, bf16[512,256]{1,0:T(8,128)(2,1)}, f32[256,128]{1,0:T(8,128)}) custom-call(bf16[1024,128]{1,0:T(8,128)(2,1)} %get-tuple-element.48.kg_ref, bf16[1024,128]{1,0:T(8,128)(2,1)} %get-tuple-element.49.conv_ref, bf16[1024,128]{1,0:T(8,128)(2,1)} %get-tuple-element.50.corr_ref, ...), custom_call_target="tpu_custom_call" | custom-call | tf_op jit(solution)/shard_map/post/pallas_call | solution.py:462
  80.0 28.5 %reduce_params.1 = (f32[64,256]{1,0:T(8,128)}, f32[1,256]{1,0:T(1,128)}, f32[1,256]{1,0:T(1,128)}, f32[33,64]{1,0:T(8,128)}, f32[64,64]{1,0:T(8,128)}, /*index=5*/f32[1,64]{1,0:T(1,128)}) custom-call(f32[256,128]{1,0:T(8,128)} %get-tuple-element.62.pack_ref), custom_call_target="tpu_custom_call" | custom-call | tf_op jit(solution)/shard_map/reduce_params/pallas_call | solution.py:414
  108.5 0.0 copy-start.3
  108.5 0.7 copy-done.3
  109.2 0.0 copy-start.2
  109.2 0.6 copy.29
  109.7 0.1 copy-done.2
  109.9 0.6 copy.30
  110.4 0.0 copy-start.1
  110.4 1.5 %copy.31 = f32[64,256]{1,0:T(8,128)} copy(f32[64,256]{1,0:T(8,128)} %get-tuple-element.83) | data formatting | bytes 131072
  111.9 0.0 copy-done.1
  111.9 0.0 copy-start
  111.9 0.6 copy.32
  112.5 0.2 copy-done
  112.7 0.0 copy-start.4
  112.7 0.6 copy.33
  113.3 0.0 copy-done.4
  113.3 0.5 copy.34
Async XLA Ops:
  108.5 0.7 copy-start.3
  109.2 0.7 copy-start.2
  110.4 1.5 %copy-start.1 = (f32[33,64]{1,0:T(8,128)S(1)}, f32[33,64]{1,0:T(8,128)}, u32[]{:S(2)}) copy-start(f32[33,64]{1,0:T(8,128)} %get-tuple-element.84) | copy-start | bytes 25348
  111.9 0.8 copy-start
  112.7 0.6 copy-start.4

commit v2 on v1

v2 whole, which is shorter than its diff:
```python
import math
from functools import partial

import jax
import jax.numpy as jnp
import ml_dtypes
import numpy as np
from jax import lax
from jax.experimental import pallas as pl
from jax.experimental.pallas import tpu as pltpu
from jax.sharding import PartitionSpec as P

MESH = pl.DeviceIdType.MESH
HIGH = lax.Precision.HIGHEST
F32 = jnp.float32
BF16 = jnp.bfloat16

SHARDS = 64
LOC = 512
CH = 256
SEQ = SHARDS * LOC
GROUP = CH // SHARDS
QUARTERS = LOC // 128
CHUNK = GROUP * QUARTERS
ROWS = SHARDS * CHUNK
LEAD, TAIL = 256, 128
ORDER, BANDS = 64, 16
MODULUS, STRIDE = 4093, 255
OWNERS = 16
PART = 16
SCALE = 1.0 / math.sqrt(SEQ)

VM = pl.BlockSpec(memory_space=pltpu.VMEM)


def split_bf16(table):
    high = table.astype(np.float32).astype(ml_dtypes.bfloat16)
    low = (table - high.astype(np.float64)).astype(np.float32).astype(ml_dtypes.bfloat16)
    return np.stack([high, low])


def transform_tables():
    lead = np.arange(LEAD)
    tail = np.arange(TAIL)
    ang1 = 2 * np.pi * ((4 * lead[:, None] + 1) * lead[None, :] % (4 * LEAD)) / (4 * LEAD)
    first = np.concatenate([np.cos(ang1), -np.sin(ang1)], axis=0)
    last = np.concatenate([np.cos(ang1).T, -np.sin(ang1).T], axis=1)
    ang2 = 2 * np.pi * (tail[:, None] * tail[None, :] % TAIL) / TAIL
    cos2, sin2 = np.cos(ang2), np.sin(ang2)
    fwd2 = np.block([[cos2, -sin2], [sin2, cos2]])
    inv2 = np.block([[cos2, sin2], [-sin2, cos2]])
    angt = 2 * np.pi * ((4 * lead[:, None] + 1) * tail[None, :]) / (4 * SEQ)
    turn = np.stack([np.cos(angt), np.sin(angt)]).astype(np.float32)
    return tuple(split_bf16(t) for t in (first, last, fwd2, inv2)) + (turn,)


def dot_t(left, right, dims, precision=HIGH):
    return lax.dot_general(
        left, right, (dims, ((), ())), precision=precision, preferred_element_type=F32
    )


def column(row):
    size = row.shape[1]
    r = lax.broadcasted_iota(jnp.int32, (size, size), 0)
    c = lax.broadcasted_iota(jnp.int32, (size, size), 1)
    return jnp.sum(jnp.where(r == c, row, 0.0), axis=1, keepdims=True)


def spread(blocks, wide, out):
    for q in range(QUARTERS):
        block = blocks(q)
        for j in range(GROUP):
            wide[pl.ds(GROUP * q + j, SHARDS, stride=CHUNK), :] = block[
                SHARDS * j : SHARDS * (j + 1)
            ]
    out[...] = wide[...].astype(BF16)


def gather_quarter(wide, q):
    return jnp.concatenate(
        [wide[pl.ds(GROUP * q + j, SHARDS, stride=CHUNK), :] for j in range(GROUP)], axis=0
    )


ANY = pl.BlockSpec(memory_space=pl.ANY)


def relative(me, dz, dy, dc):
    z, y, c = lax.div(me, 8), lax.rem(lax.div(me, 2), 4), lax.rem(me, 2)
    return (lax.rem(z + dz, 8) * 4 + lax.rem(y + dy, 4)) * 2 + lax.rem(c + dc, 2)


def far_first(me, i):
    left = 63 - i
    m = lax.rem(left, 8)
    dz = jnp.where(lax.rem(m, 2) == 1, lax.div(m + 1, 2), lax.rem(8 - lax.div(m, 2), 8))
    return relative(me, dz, lax.rem(lax.div(left, 8), 4), lax.div(left, 32))


def main_kernel(
    sig_hbm, gate_hbm, cot_hbm, gain_ref, logr_ref, emb_ref, freq_ref, mid_ref, outw_ref,
    first_hbm, last_hbm, fwd2_hbm, inv2_hbm, turn_hbm,
    out_ref, sgrad_ref, ggrad_ref, total_ref,
    sig_ref, gate_ref, cot_ref, first_ref, last_ref, fwd2_ref, inv2_ref, turn_ref,
    wide, emb_pad, env_ref, raw_ref, feat_ref, mid_buf, spec_s, spec_u, spec_k,
    sends, recvs, pack32, pack16, parts, mine_buf, cross, total16,
    load_sem, send_sem, recv_sem, own_sem, sums_sem,
):
    me = lax.axis_index("seq")
    lane = lax.axis_index("ch")
    others = [lax.rem(lane + i, 4) for i in (1, 2, 3)]
    barrier = pltpu.get_barrier_semaphore()

    def greet(i, carry):
        pl.semaphore_signal(
            barrier, inc=1, device_id={"seq": lax.rem(me + i, SHARDS)}, device_id_type=MESH
        )
        return carry

    lax.fori_loop(1, SHARDS, greet, 0)
    for peer in others:
        pl.semaphore_signal(barrier, inc=1, device_id={"ch": peer}, device_id_type=MESH)

    loads = [
        pltpu.make_async_copy(a, b, load_sem.at[n])
        for n, (a, b) in enumerate(
            (
                (sig_hbm, sig_ref), (gate_hbm, gate_ref), (cot_hbm, cot_ref), (first_hbm, first_ref),
                (turn_hbm, turn_ref), (fwd2_hbm, fwd2_ref), (inv2_hbm, inv2_ref), (last_hbm, last_ref),
            )
        )
    ]
    for load in loads:
        load.start()

    mine = pl.ds(pl.multiple_of(me * CHUNK, CHUNK), CHUNK)

    def push(f):
        def one(i, carry):
            peer = far_first(me, i)
            theirs = pl.ds(pl.multiple_of(peer * CHUNK, CHUNK), CHUNK)
            pltpu.make_async_remote_copy(
                src_ref=sends.at[f, theirs],
                dst_ref=recvs.at[f, mine],
                send_sem=send_sem.at[f],
                recv_sem=recv_sem.at[f],
                device_id={"seq": peer},
                device_id_type=MESH,
            ).start()
            return carry

        lax.fori_loop(0, SHARDS - 1, one, 0)
        pltpu.make_async_copy(sends.at[f, mine], recvs.at[f, mine], own_sem.at[f]).start()

    def all_of(f):
        rest = pl.ds(0, ROWS - CHUNK)
        return pltpu.make_async_remote_copy(
            src_ref=sends.at[f, rest],
            dst_ref=recvs.at[f, rest],
            send_sem=send_sem.at[f],
            recv_sem=recv_sem.at[f],
            device_id={"seq": me},
            device_id_type=MESH,
        )

    def arrive(f):
        pltpu.make_async_copy(sends.at[f, mine], recvs.at[f, mine], own_sem.at[f]).wait()
        all_of(f).wait_recv()

    loads[0].wait()
    spread(lambda q: jnp.transpose(sig_ref[128 * q : 128 * (q + 1)].astype(F32)), wide, sends.at[0])
    loads[1].wait()
    loads[2].wait()

    def upstream(rows):
        return (cot_ref[rows].astype(F32) * gate_ref[rows].astype(F32)).astype(BF16).astype(F32)

    spread(lambda q: jnp.transpose(upstream(slice(128 * q, 128 * (q + 1)))), wide, sends.at[1])
    pl.semaphore_wait(barrier, SHARDS - 1 + len(others))
    push(0)
    push(1)

    base = me * LOC
    band = 1 + STRIDE * lax.broadcasted_iota(jnp.int32, (BANDS, LOC), 0)
    prod = (base + lax.broadcasted_iota(jnp.int32, (BANDS, LOC), 1)) * band
    quot = (prod.astype(F32) * (1.0 / MODULUS)).astype(jnp.int32)
    rem = prod - quot * MODULUS
    rem = jnp.where(rem < 0, rem + MODULUS, rem)
    rem = jnp.where(rem >= MODULUS, rem - MODULUS, rem)
    angle = rem.astype(F32) * (2.0 * math.pi / MODULUS)
    place = (base + lax.broadcasted_iota(jnp.int32, (1, LOC), 1)).astype(F32)
    feat_ref[...] = jnp.zeros_like(feat_ref)
    feat_ref[0:1, :] = place / SEQ
    feat_ref[1 : 1 + BANDS, :] = jnp.cos(angle)
    feat_ref[1 + BANDS : 1 + 2 * BANDS, :] = jnp.sin(angle)
    emb_pad[...] = jnp.zeros_like(emb_pad)
    emb_pad[0 : 1 + 2 * BANDS, :] = emb_ref[...]
    freq = column(freq_ref[...])
    h1 = dot_t(emb_pad[...], feat_ref[...], ((0,), (0,)))
    a1 = jnp.sin(freq * h1)
    h2 = dot_t(mid_ref[...], a1, ((0,), (0,)))
    a2 = jnp.sin(freq * h2)
    raw = dot_t(outw_ref[...], a2, ((0,), (0,)))
    rate = jnp.exp(column(logr_ref[...]))
    env = jnp.exp(-rate * place) * jnp.sqrt(2.0 * rate)
    env_ref[...] = env
    raw_ref[...] = raw * (0.5 - rate * place)
    kern = raw * env
    spread(lambda q: kern[:, 128 * q : 128 * (q + 1)], wide, sends.at[2])
    push(2)

    def dot2(left_pair, right):
        return jnp.dot(left_pair[0], right, preferred_element_type=F32) + jnp.dot(
            left_pair[1], right, preferred_element_type=F32
        )

    def forward(f, spec):
        wide[...] = recvs[f].astype(F32)
        seqs = jnp.concatenate(
            [wide[pl.ds(j, LEAD, stride=GROUP), :].astype(BF16) for j in range(GROUP)], axis=1
        )
        cos, sin = turn_ref[0], turn_ref[1]
        step = dot2((first_ref[0], first_ref[1]), seqs)
        for j in range(GROUP):
            re = step[:LEAD, TAIL * j : TAIL * (j + 1)]
            im = step[LEAD:, TAIL * j : TAIL * (j + 1)]
            mid_buf[LEAD * j : LEAD * (j + 1), :TAIL] = (re * cos + im * sin).astype(BF16)
            mid_buf[LEAD * j : LEAD * (j + 1), TAIL:] = (im * cos - re * sin).astype(BF16)
        turned = mid_buf[...]
        spec[...] = jnp.dot(turned, fwd2_ref[0], preferred_element_type=F32) + jnp.dot(
            turned, fwd2_ref[1], preferred_element_type=F32
        )

    def inverse(left, right, conj_left, f):
        lr, li = left[:, :TAIL], left[:, TAIL:]
        rr, ri = right[:, :TAIL], right[:, TAIL:]
        if conj_left:
            re, im = lr * rr + li * ri, lr * ri - li * rr
        else:
            re, im = lr * rr - li * ri, lr * ri + li * rr
        mid_buf[:, :TAIL] = re.astype(BF16)
        mid_buf[:, TAIL:] = im.astype(BF16)
        spec = mid_buf[...]
        step = jnp.dot(spec, inv2_ref[0], preferred_element_type=F32) + jnp.dot(
            spec, inv2_ref[1], preferred_element_type=F32
        )
        cos, sin = turn_ref[0], turn_ref[1]
        reals, imags = [], []
        for j in range(GROUP):
            re = step[LEAD * j : LEAD * (j + 1), :TAIL]
            im = step[LEAD * j : LEAD * (j + 1), TAIL:]
            reals.append((re * cos - im * sin).astype(BF16))
            imags.append((im * cos + re * sin).astype(BF16))
        both = jnp.concatenate(
            [jnp.concatenate(reals, axis=1), jnp.concatenate(imags, axis=1)], axis=0
        )
        field = dot2((last_ref[0], last_ref[1]), both) * (1.0 / SEQ)
        for j in range(GROUP):
            wide[pl.ds(j, LEAD, stride=GROUP), :] = field[:, TAIL * j : TAIL * (j + 1)]
        sends[f] = wide[...].astype(BF16)

    for load in loads[3:]:
        load.wait()
    arrive(0)
    forward(0, spec_s)
    arrive(1)
    forward(1, spec_u)
    inverse(spec_s, spec_u, True, 3)
    push(3)
    arrive(2)
    forward(2, spec_k)
    inverse(spec_k, spec_s, False, 4)
    push(4)
    inverse(spec_k, spec_u, True, 5)

    skip = jnp.zeros((1, CH), F32)
    for q in range(QUARTERS):
        rows = slice(128 * q, 128 * (q + 1))
        skip = skip + jnp.sum(sig_ref[rows].astype(F32) * upstream(rows), axis=0, keepdims=True)
    cos1, cos2 = jnp.cos(freq * h1), jnp.cos(freq * h2)
    arrive(3)
    wide[...] = recvs[3].astype(F32)
    kgrad = jnp.concatenate([gather_quarter(wide, q) for q in range(QUARTERS)], axis=1)
    scaled = kgrad * env_ref[...]
    ones = jnp.ones((8, LOC), F32)
    rate_part = dot_t(ones, scaled * raw_ref[...], ((1,), (1,)))[0:1]
    out_part = dot_t(a2, scaled, ((1,), (1,)))
    g2 = jnp.dot(outw_ref[...], scaled, precision=HIGH, preferred_element_type=F32)
    c2 = cos2 * g2
    d2 = freq * c2
    mid_part = dot_t(a1, d2, ((1,), (1,)))
    c1 = cos1 * jnp.dot(mid_ref[...], d2, precision=HIGH, preferred_element_type=F32)
    emb_part = dot_t(feat_ref[...], freq * c1, ((1,), (1,)))
    freq_part = dot_t(ones, c2 * h2 + c1 * h1, ((1,), (1,)))[0:1]

    pack32[pl.ds(0, 64, stride=4), :] = out_part[:, :128]
    pack32[pl.ds(1, 64, stride=4), :] = out_part[:, 128:]
    emb_cols = jnp.concatenate(
        [emb_part, jnp.broadcast_to(freq_part, (8, ORDER)), jnp.zeros((16, ORDER), F32)], axis=0
    )
    pack32[pl.ds(2, 64, stride=4), :] = jnp.concatenate([mid_part, emb_cols], axis=1)
    pack32[pl.ds(3, 64, stride=4), :] = jnp.zeros((64, 128), F32)
    pack32[3:4, :] = skip[:, :128]
    pack32[7:8, :] = skip[:, 128:]
    pack32[11:12, :] = rate_part[:, :128]
    pack32[15:16, :] = rate_part[:, 128:]
    pack16[...] = pack32[...].astype(BF16)

    slot_of = lax.div(me, 4)
    is_owner = lax.rem(me, 4) == 0
    own_rows = pl.ds(pl.multiple_of(slot_of * PART, PART), PART)

    def hand_in(i, carry):
        slot = lax.rem(slot_of + i, OWNERS)
        pltpu.make_async_remote_copy(
            src_ref=pack16.at[pl.ds(pl.multiple_of(slot * PART, PART), PART)],
            dst_ref=parts.at[me],
            send_sem=sums_sem.at[0],
            recv_sem=sums_sem.at[1],
            device_id={"seq": 4 * slot},
            device_id_type=MESH,
        ).start()
        return carry

    lax.fori_loop(1, OWNERS, hand_in, 0)

    @pl.when(jnp.logical_not(is_owner))
    def _():
        hand_in(0, 0)

    push(5)

    def sums(n, send, recv):
        return pltpu.make_async_remote_copy(
            src_ref=parts.at[pl.ds(0, n)],
            dst_ref=parts.at[pl.ds(0, n)],
            send_sem=sums_sem.at[send],
            recv_sem=sums_sem.at[recv],
            device_id={"seq": me},
            device_id_type=MESH,
        )

    gain = gain_ref[...]
    arrive(4)
    wide[...] = recvs[4].astype(F32)
    for q in range(QUARTERS):
        rows = slice(128 * q, 128 * (q + 1))
        mixed = jnp.transpose(gather_quarter(wide, q)) + gain * sig_ref[rows].astype(F32)
        out_ref[rows] = (gate_ref[rows].astype(F32) * mixed).astype(BF16)
        ggrad_ref[rows] = (cot_ref[rows].astype(F32) * mixed).astype(BF16)

    @pl.when(is_owner)
    def _():
        sums(SHARDS - 1, 0, 1).wait_recv()
        parts[me] = pack16[own_rows]
        acc = parts[0].astype(F32)
        for s in range(1, SHARDS):
            acc = acc + parts[s].astype(F32)
        mine_buf[...] = acc
        for n, other in enumerate(others):
            pltpu.make_async_remote_copy(
                src_ref=mine_buf,
                dst_ref=cross.at[2 - n],
                send_sem=sums_sem.at[2],
                recv_sem=sums_sem.at[3],
                device_id={"ch": other},
                device_id_type=MESH,
            ).start()
        three = pltpu.make_async_remote_copy(
            src_ref=cross,
            dst_ref=cross,
            send_sem=sums_sem.at[2],
            recv_sem=sums_sem.at[3],
            device_id={"seq": me},
            device_id_type=MESH,
        )
        three.wait_recv()
        shared = lax.rem(lax.broadcasted_iota(jnp.int32, (PART, 128), 0), 4) == 2
        acc = acc + jnp.where(shared, cross[0] + cross[1] + cross[2], 0.0)
        total16[own_rows] = acc.astype(BF16)

        def tell(i, carry):
            pltpu.make_async_remote_copy(
                src_ref=total16.at[own_rows],
                dst_ref=total16.at[own_rows],
                send_sem=sums_sem.at[4],
                recv_sem=sums_sem.at[5],
                device_id={"seq": far_first(me, i)},
                device_id_type=MESH,
            ).start()
            return carry

        lax.fori_loop(0, SHARDS - 1, tell, 0)
        three.wait_send()

    arrive(5)
    wide[...] = recvs[5].astype(F32)
    for q in range(QUARTERS):
        rows = slice(128 * q, 128 * (q + 1))
        corr = jnp.transpose(gather_quarter(wide, q))
        sgrad_ref[rows] = (gain * upstream(rows) + corr).astype(BF16)

    for f in range(6):
        all_of(f).wait_send()

    @pl.when(is_owner)
    def _():
        sums(OWNERS - 1, 4, 5).wait_recv()
        sums(SHARDS - 1, 4, 5).wait_send()
        sums(OWNERS - 1, 0, 1).wait_send()

    @pl.when(jnp.logical_not(is_owner))
    def _():
        sums(OWNERS, 0, 1).wait_send()
        sums(OWNERS, 4, 5).wait_recv()

    total_ref[...] = total16[...].astype(F32) * SCALE


def unpack_kernel(total, out_ref, skip_ref, rate_ref, emb_ref, mid_ref, freq_ref):
    out_ref[:, :128] = total[pl.ds(0, 64, stride=4), :]
    out_ref[:, 128:] = total[pl.ds(1, 64, stride=4), :]
    shared_rows = total[pl.ds(2, 64, stride=4), :]
    mid_ref[...] = shared_rows[:, :ORDER]
    emb_ref[...] = shared_rows[: 1 + 2 * BANDS, ORDER:]
    freq_ref[...] = shared_rows[40:41, ORDER:]
    skip_ref[:, :128] = total[3:4, :]
    skip_ref[:, 128:] = total[7:8, :]
    rate_ref[:, :128] = total[11:12, :]
    rate_ref[:, 128:] = total[15:16, :]


def on_device(signal, gate_values, cotangent, skip_gain, log_rate, embed_weight, sine_freq, mid_weight, out_weight):
    tables = transform_tables()
    wide_out = jax.ShapeDtypeStruct((LOC, CH), BF16)
    output, signal_grad, gate_grad, total = pl.pallas_call(
        main_kernel,
        out_shape=[wide_out] * 3 + [jax.ShapeDtypeStruct((256, 128), F32)],
        in_specs=[ANY] * 3 + [VM] * 6 + [ANY] * 5,
        out_specs=[VM] * 4,
        scratch_shapes=[pltpu.VMEM((LOC, CH), BF16)] * 3
        + [pltpu.VMEM(t.shape, t.dtype) for t in tables]
        + [
            pltpu.VMEM((ROWS, 128), F32),
            pltpu.VMEM((40, ORDER), F32),
            pltpu.VMEM((CH, LOC), F32),
            pltpu.VMEM((CH, LOC), F32),
            pltpu.VMEM((40, LOC), F32),
            pltpu.VMEM((ROWS, 256), BF16),
            pltpu.VMEM((ROWS, 256), F32),
            pltpu.VMEM((ROWS, 256), F32),
            pltpu.VMEM((ROWS, 256), F32),
            pltpu.VMEM((6, ROWS, 128), BF16),
            pltpu.VMEM((6, ROWS, 128), BF16),
            pltpu.VMEM((256, 128), F32),
            pltpu.VMEM((256, 128), BF16),
            pltpu.VMEM((SHARDS, PART, 128), BF16),
            pltpu.VMEM((PART, 128), F32),
            pltpu.VMEM((3, PART, 128), F32),
            pltpu.VMEM((256, 128), BF16),
            pltpu.SemaphoreType.DMA((8,)),
            pltpu.SemaphoreType.DMA((6,)),
            pltpu.SemaphoreType.DMA((6,)),
            pltpu.SemaphoreType.DMA((6,)),
            pltpu.SemaphoreType.DMA((6,)),
        ],
        compiler_params=pltpu.CompilerParams(collective_id=1, has_side_effects=True),
        name="hyena",
    )(
        signal, gate_values, cotangent, skip_gain[None, :], log_rate[None, :], embed_weight,
        sine_freq[None, :], mid_weight, out_weight, *tables,
    )
    shapes = [(ORDER, CH), (1, CH), (1, CH), (1 + 2 * BANDS, ORDER), (ORDER, ORDER), (1, ORDER)]
    out_sum, skip_sum, rate_sum, emb_sum, mid_sum, freq_sum = pl.pallas_call(
        unpack_kernel,
        out_shape=[jax.ShapeDtypeStruct(s, F32) for s in shapes],
        in_specs=[VM],
        out_specs=[VM] * len(shapes),
        name="unpack",
    )(total)
    return (
        output, signal_grad, gate_grad, skip_sum[0], rate_sum[0], out_sum, emb_sum, mid_sum, freq_sum[0],
    )


def solution(mesh):
    wide, flat, rep = P("seq", "ch"), P("ch"), P()
    return jax.shard_map(
        on_device,
        mesh=mesh,
        in_specs=(wide, wide, wide, flat, flat, rep, rep, rep, P(None, "ch")),
        out_specs=(wide, wide, wide, flat, flat, P(None, "ch"), rep, rep, rep),
        check_vma=False,
    )
```

time: 114 us -> 65.3 us (0.57)
  Pallas kernels: 108 us -> 60.9 us
  local copies, waits for them, and re-layouts: 5.29 us -> 3.46 us
    pallas_call x6 -> x2, Pallas kernels: 108 us -> 60.9 us  [the longest x1 59.3 us: on_device(): pl.pallas_call(main_kernel, out_shape=[wide_out] * 3 + [jax.ShapeDtypeStr...]
    unnamed x16 -> x7, local copies, waits for them, and re-layouts: 5.29 us -> 3.46 us
where the time goes in v2:
time: 65.3 us; the launch traced here: 65.1 us
  Pallas kernels  60.9 us (93%)
  local copies, waits for them, and re-layouts  3.46 us (5%)
  between operations  0.66 us (1%)
    pallas_call x1, Pallas kernels, on_device(): pl.pallas_call(main_kernel, out_shape=[wide_out] * 3 + [jax.ShapeDtypeStr...  59.3 us
    unnamed x7, local copies, waits for them, and re-layouts  3.46 us
    pallas_call x1, Pallas kernels, on_device(): pl.pallas_call(unpack_kernel, out_shape=[jax.ShapeDtypeStruct(s, F32) for...  1.6 us

profile of v2, /device:TPU:1, one launch (start us, length us, event | category | flops | bytes accessed | tf_op | source)
XLA Modules:
  0.0 65.1 jit_solution(14219299853607852254)
XLA Ops:
  0.6 59.3 %hyena.1 = (bf16[512,256]{1,0:T(8,128)(2,1)}, bf16[512,256]{1,0:T(8,128)(2,1)}, bf16[512,256]{1,0:T(8,128)(2,1)}, f32[256,128]{1,0:T(8,128)}) custom-call(bf16[512,256]{1,0:T(8,128)(2,1)} %sig_hbm.1, bf16[512,256]{1,0:T(8,128)(2,1)} %gate_hbm.1, bf16[512,256]{1,0:T(8,128)(2,1)} %cot_hbm.1, f32[1,256]{1,0:T(1,128)} %bitcast.6, f32[1,256]{1,0:T(1,128)} %bitcast.7, ...), custom_call_target="tpu_custom_call" | custom-call | tf_op jit(solution)/shard_map/hyena/pallas_call | solution.py:437
  60.0 1.6 %unpack.1 = (f32[64,256]{1,0:T(8,128)}, f32[1,256]{1,0:T(1,128)}, f32[1,256]{1,0:T(1,128)}, f32[33,64]{1,0:T(8,128)}, f32[64,64]{1,0:T(8,128)}, /*index=5*/f32[1,64]{1,0:T(1,128)}) custom-call(f32[256,128]{1,0:T(8,128)} %get-tuple-element.22.total), custom_call_target="tpu_custom_call" | custom-call | tf_op jit(solution)/shard_map/unpack/pallas_call | solution.py:475
  61.6 0.0 copy-start.1
  61.6 1.7 %copy.26 = bf16[512,256]{1,0:T(8,128)(2,1)} copy(bf16[512,256]{1,0:T(8,128)(2,1)} %get-tuple-element.38) | data formatting | bytes 524288
  63.3 0.0 copy-done.1
  63.3 0.0 copy-start
  63.3 0.7 %copy.27 = bf16[512,256]{1,0:T(8,128)(2,1)} copy(bf16[512,256]{1,0:T(8,128)(2,1)S(1)} %copy-done.1) | data formatting | bytes 524288
  64.0 0.3 copy-done
  64.3 0.7 %copy.28 = bf16[512,256]{1,0:T(8,128)(2,1)} copy(bf16[512,256]{1,0:T(8,128)(2,1)S(1)} %copy-done) | data formatting | bytes 524288
Async XLA Ops:
  61.6 1.7 %copy-start.1 = (bf16[512,256]{1,0:T(8,128)(2,1)S(1)}, bf16[512,256]{1,0:T(8,128)(2,1)}, u32[]{:S(2)}) copy-start(bf16[512,256]{1,0:T(8,128)(2,1)} %get-tuple-element.39) | copy-start | bytes 786436
  63.3 1.0 %copy-start = (bf16[512,256]{1,0:T(8,128)(2,1)S(1)}, bf16[512,256]{1,0:T(8,128)(2,1)}, u32[]{:S(2)}) copy-start(bf16[512,256]{1,0:T(8,128)(2,1)} %get-tuple-element.40) | copy-start | bytes 786436
